TPU v7x, 256 devices: a whole 4x4x8 slice. The times are simulated.
256 devices in a mesh: gx: 64 (over y, z, core), gy: 4 (over x).
Axes of the slice: x: 4, y: 4, z: 8, core: 2. Of those that a mesh axis runs over, the one named last changes fastest.
Arguments:
- members_state: float32 [3, 64, 512, 512], P(None, None, 'gx', 'gy'), may hold values from -6 to 6
- depth_level: int32 [512, 512], P('gx', 'gy'), may hold values from 1 to 8
- land_mask: int32 [512, 512], P('gx', 'gy'), may hold values 0 or 1
- obs_cells: int32 [64, 4, 256], P('gx', 'gy'), may hold values from 0 to 1023
- obs_values: float32 [64, 4, 256], P('gx', 'gy'), may hold values from -6 to 6
- obs_error: float32 [64, 4, 256], P('gx', 'gy'), may hold values from 2 to 8
Outputs:
- analysis: float32 [3, 64, 512, 512], P(None, None, 'gx', 'gy')
Inputs may be any that keep to these rules, and one draw needn't show every extreme that they name: Each value of obs_cells is the row-major index of a cell within the 8 x 128 block held by the device at the same position along gx and gy.
All inputs are finite; a program needn't handle non-finite values. No bound on the sum of `land_mask` on one device may be relied on, other than what follows from the above.
Results may differ from a plain program's by a relative error of at most 0.00005.
Values sent between devices are 32-bit elements; how exact they have to be, the bound alone decides.
No kernel may reach another device: no remote copies, remote signals or barrier semaphores. Data moves between devices by JAX's collectives and lax.ppermute only.
A program may use at most 64 MiB of HBM per device.

v0:
```python
import jax
import jax.numpy as jnp
from jax import lax
from jax.sharding import PartitionSpec as P


def extended(block, sides, width):
    for axis, dim in sides:
        count = lax.axis_size(axis)
        forward = [(i, i + 1) for i in range(count - 1)]
        backward = [(target, source) for source, target in forward]
        low = lax.ppermute(
            lax.slice_in_dim(block, block.shape[dim] - width, None, axis=dim), axis, forward
        )
        high = lax.ppermute(lax.slice_in_dim(block, 0, width, axis=dim), axis, backward)
        block = jnp.concatenate([low, block, high], axis=dim)
    return block


def height_tendency(padded, geo):
    h = padded[0]
    u = padded[1]
    v = padded[2]
    depth = geo[0]
    mask = geo[1][1:-1, 1:-1]
    east = depth * u
    north = depth * v

    def along_x(a):
        return (a[:, 2:, 1:-1] - a[:, :-2, 1:-1]) * 0.5

    def along_y(a):
        return (a[:, 1:-1, 2:] - a[:, 1:-1, :-2]) * 0.5

    def laplace(a):
        return (
            a[:, 2:, 1:-1]
            + a[:, :-2, 1:-1]
            + a[:, 1:-1, 2:]
            + a[:, 1:-1, :-2]
            - 4.0 * a[:, 1:-1, 1:-1]
        )

    def inner(a):
        return a[:, 1:-1, 1:-1]

    dh = -along_x(east) - along_y(north) + 0.05 * laplace(h)
    du = -along_x(h) + 0.2 * inner(v) + 0.05 * laplace(u)
    dv = -along_y(h) - 0.2 * inner(u) + 0.05 * laplace(v)
    return jnp.stack([dh, du, dv]) * mask


def tri_solve(lower, rhs, flipped):
    return lax.linalg.triangular_solve(lower, rhs, left_side=True, lower=True, transpose_a=flipped)


def padded_section(field):
    return extended(field, (("gx", 2), ("gy", 3)), 1)


def local(members_state, depth_level, land_mask, obs_cells, obs_values, obs_error):
    maskf = land_mask.astype(jnp.float32)
    geo = jnp.stack([0.25 * depth_level.astype(jnp.float32) * maskf, maskf])
    geo_wide = extended(geo, (("gx", 1), ("gy", 2)), 3)
    first_offset = members_state * maskf
    single_geometry = geo_wide[:, 2:-2, 2:-2]
    s1 = first_offset + 0.3 * height_tendency(padded_section(first_offset), single_geometry)
    variance_estimate2 = 0.75 * first_offset + 0.25 * (
        s1 + 0.3 * height_tendency(padded_section(s1), single_geometry)
    )
    prior_model_vector = 1.0 / 3.0 * first_offset + 2.0 / 3.0 * (
        variance_estimate2
        + 0.3 * height_tendency(padded_section(variance_estimate2), single_geometry)
    )
    sample_average = jnp.mean(prior_model_vector, axis=1, keepdims=True)
    sample_deviations = prior_model_vector - sample_average
    sample_number = prior_model_vector.shape[1]
    free_elevation_field = prior_model_vector[0].reshape(sample_number, -1)
    measured_data = jnp.take(free_elevation_field, obs_cells.reshape(-1), axis=1)
    obs_mean = jnp.mean(measured_data, axis=0, keepdims=True)
    error = obs_error.reshape(-1)
    scaled = (measured_data - obs_mean) / (error * jnp.sqrt(jnp.float32(sample_number - 1)))
    innovation = (obs_values.reshape(-1) - obs_mean[0]) / error
    gram_part = jnp.dot(scaled, scaled.T, precision=lax.Precision.HIGHEST)
    proj_part = jnp.dot(scaled, innovation, precision=lax.Precision.HIGHEST)
    eye = jnp.eye(sample_number, dtype=jnp.float32)
    gram, projection = lax.psum((gram_part, proj_part), ("gx", "gy"))
    lower = jnp.linalg.cholesky(eye + gram)
    half = tri_solve(lower, projection[:, None], False)
    weights = tri_solve(lower, half, True)[:, 0]
    inverse = tri_solve(lower, eye, False)
    transform = weights[:, None] / jnp.sqrt(jnp.float32(sample_number - 1)) + inverse.T
    mixed = jnp.einsum(
        "km,fkxy->fmxy", transform, sample_deviations, precision=lax.Precision.HIGHEST
    )
    return sample_average + mixed


def solution(mesh):
    placed = (
        P(None, None, "gx", "gy"),
        P("gx", "gy"),
        P("gx", "gy"),
        P("gx", "gy", None),
        P("gx", "gy", None),
        P("gx", "gy", None),
    )
    return jax.shard_map(
        local, mesh=mesh, in_specs=placed, out_specs=P(None, None, "gx", "gy"), check_vma=False
    )
```

profile of v0, /device:TPU:1, one launch (start us, length us, event | category | flops | bytes accessed | tf_op | source)
XLA Modules:
  0.0 180.3 jit_solution(6452280479091019301)
XLA Ops:
  1.4 5.1 %collective-permute-start.1 = (f32[2,3,128]{2,1,0:T(4,128)S(1)}, f32[2,3,128]{2,1,0:T(4,128)S(1)}, u32[]{:S(2)}, u32[]{:S(2)}) collective-permute-start(f32[2,3,128]{2,1,0:T(4,128)S(1)} %get-tuple-element.47), channel_id=1, source_target_pairs={{4,0},{8,4},{12,8},{16,12},{20,16},{24,20},{28,24},{32,28},{36,32}... | collective-permute-start | bytes 9224 | tf_op jit(solution)/shard_map/ppermute | solution.py:15
  6.5 1.9 %collective-permute-start = (f32[2,3,128]{2,1,0:T(4,128)S(1)}, f32[2,3,128]{2,1,0:T(4,128)S(1)}, u32[]{:S(2)}, u32[]{:S(2)}) collective-permute-start(f32[2,3,128]{2,1,0:T(4,128)S(1)} %get-tuple-element.46), channel_id=1, source_target_pairs={{0,4},{4,8},{8,12},{12,16},{16,20},{20,24},{24,28},{28,32},{32,36}... | collective-permute-start | bytes 9224 | tf_op jit(solution)/shard_map/ppermute | solution.py:12
  8.4 1.6 copy.15
  11.7 4.0 %collective-permute-start.2 = (f32[2,14,3]{2,1,0:T(8,128)S(1)}, f32[2,14,3]{2,1,0:T(8,128)S(1)}, u32[]{:S(2)}, u32[]{:S(2)}) collective-permute-start(f32[2,14,3]{2,1,0:T(8,128)S(1)} %get-tuple-element.44), channel_id=1, source_target_pairs={{0,1},{1,2},{2,3},{4,5},{5,6},{6,7},{8,9},{9,10},{10,11},{12,13},{... | collective-permute-start | bytes 1016 | tf_op jit(solution)/shard_map/ppermute | solution.py:12
  15.7 3.0 %collective-permute-start.5 = (f32[3,64,1,128]{1,3,2,0:T(8,128)S(1)}, f32[3,64,1,128]{1,3,2,0:T(8,128)S(1)}, u32[]{:S(2)}, u32[]{:S(2)}) collective-permute-start(f32[3,64,1,128]{1,3,2,0:T(8,128)S(1)} %get-tuple-element.41), channel_id=1, source_target_pairs={{4,0},{8,4},{12,8},{16,12},{20,16},{24,20},{28,24},{32,28},{36,32}... | collective-permute-start | bytes 294920 | tf_op jit(solution)/shard_map/ppermute | solution.py:15
  18.7 2.6 %collective-permute-start.4 = (f32[3,64,1,128]{1,3,2,0:T(8,128)S(1)}, f32[3,64,1,128]{1,3,2,0:T(8,128)S(1)}, u32[]{:S(2)}, u32[]{:S(2)}) collective-permute-start(f32[3,64,1,128]{1,3,2,0:T(8,128)S(1)} %get-tuple-element.40), channel_id=1, source_target_pairs={{0,4},{4,8},{8,12},{12,16},{16,20},{20,24},{24,28},{28,32},{32,36}... | collective-permute-start | bytes 294920 | tf_op jit(solution)/shard_map/ppermute | solution.py:12
  21.4 1.3 collective-permute-done.5
  23.9 1.3 collective-permute-start.7
  25.2 4.0 %collective-permute-start.6 = (f32[3,64,10,1]{1,3,2,0:T(1,128)S(1)}, f32[3,64,10,1]{1,3,2,0:T(1,128)S(1)}, u32[]{:S(2)}, u32[]{:S(2)}) collective-permute-start(f32[3,64,10,1]{1,3,2,0:T(1,128)S(1)} %get-tuple-element.34), channel_id=1, source_target_pairs={{0,1},{1,2},{2,3},{4,5},{5,6},{6,7},{8,9},{9,10},{10,11},{12,13},{... | collective-permute-start | bytes 23048 | tf_op jit(solution)/shard_map/ppermute | solution.py:12
  32.1 1.9 %collective-permute-start.9 = (f32[3,64,1,128]{1,3,2,0:T(8,128)S(1)}, f32[3,64,1,128]{1,3,2,0:T(8,128)S(1)}, u32[]{:S(2)}, u32[]{:S(2)}) collective-permute-start(f32[3,64,1,128]{1,3,2,0:T(8,128)S(1)} %get-tuple-element.39), channel_id=1, source_target_pairs={{4,0},{8,4},{12,8},{16,12},{20,16},{24,20},{28,24},{32,28},{36,32}... | collective-permute-start | bytes 294920 | tf_op jit(solution)/shard_map/ppermute | solution.py:15
  34.1 5.5 %collective-permute-start.8 = (f32[3,64,1,128]{1,3,2,0:T(8,128)S(1)}, f32[3,64,1,128]{1,3,2,0:T(8,128)S(1)}, u32[]{:S(2)}, u32[]{:S(2)}) collective-permute-start(f32[3,64,1,128]{1,3,2,0:T(8,128)S(1)} %get-tuple-element.38), channel_id=1, source_target_pairs={{0,4},{4,8},{8,12},{12,16},{16,20},{20,24},{24,28},{28,32},{32,36}... | collective-permute-start | bytes 294920 | tf_op jit(solution)/shard_map/ppermute | solution.py:12
  39.6 1.4 collective-permute-done.9
  42.2 1.3 collective-permute-start.11
  43.5 4.5 %collective-permute-start.10 = (f32[3,64,10,1]{1,3,2,0:T(1,128)S(1)}, f32[3,64,10,1]{1,3,2,0:T(1,128)S(1)}, u32[]{:S(2)}, u32[]{:S(2)}) collective-permute-start(f32[3,64,10,1]{1,3,2,0:T(1,128)S(1)} %get-tuple-element.32), channel_id=1, source_target_pairs={{0,1},{1,2},{2,3},{4,5},{5,6},{6,7},{8,9},{9,10},{10,11},{12,13},{... | collective-permute-start | bytes 23048 | tf_op jit(solution)/shard_map/ppermute | solution.py:12
  51.4 1.9 %collective-permute-start.13 = (f32[3,64,1,128]{1,3,2,0:T(8,128)S(1)}, f32[3,64,1,128]{1,3,2,0:T(8,128)S(1)}, u32[]{:S(2)}, u32[]{:S(2)}) collective-permute-start(f32[3,64,1,128]{1,3,2,0:T(8,128)S(1)} %get-tuple-element.37), channel_id=1, source_target_pairs={{4,0},{8,4},{12,8},{16,12},{20,16},{24,20},{28,24},{32,28},{36,32}... | collective-permute-start | bytes 294920 | tf_op jit(solution)/shard_map/ppermute | solution.py:15
  53.3 5.2 %collective-permute-start.12 = (f32[3,64,1,128]{1,3,2,0:T(8,128)S(1)}, f32[3,64,1,128]{1,3,2,0:T(8,128)S(1)}, u32[]{:S(2)}, u32[]{:S(2)}) collective-permute-start(f32[3,64,1,128]{1,3,2,0:T(8,128)S(1)} %get-tuple-element.36), channel_id=1, source_target_pairs={{0,4},{4,8},{8,12},{12,16},{16,20},{20,24},{24,28},{28,32},{32,36}... | collective-permute-start | bytes 294920 | tf_op jit(solution)/shard_map/ppermute | solution.py:12
  58.6 1.4 collective-permute-done.13
  62.5 4.5 %collective-permute-start.14 = (f32[3,64,10,1]{1,3,2,0:T(1,128)S(1)}, f32[3,64,10,1]{1,3,2,0:T(1,128)S(1)}, u32[]{:S(2)}, u32[]{:S(2)}) collective-permute-start(f32[3,64,10,1]{1,3,2,0:T(1,128)S(1)} %get-tuple-element.30), channel_id=1, source_target_pairs={{0,1},{1,2},{2,3},{4,5},{5,6},{6,7},{8,9},{9,10},{10,11},{12,13},{... | collective-permute-start | bytes 23048 | tf_op jit(solution)/shard_map/ppermute | solution.py:12
  69.5 1.7 fusion.77
  73.0 91.1 %all-reduce = (f32[64,64]{1,0:T(8,128)S(1)}, f32[64]{0:T(128)S(1)}) all-reduce(f32[64,64]{1,0:T(8,128)S(1)} %fusion.83, f32[64]{0:T(128)S(1)} %convolution_bitcast_fusion.2), channel_id=1, replica_groups=mesh['gx'=64,'gy'=4] {'gx','gy'}, use_global_device_ids=true, to_apply=%region_2.3 | all-reduce | flops 4160 | bytes 33280 | tf_op jit(solution)/shard_map/psum | solution.py:87
  164.2 5.8 %cholesky.18 = f32[64,64]{1,0:T(8,128)S(1)} custom-call(f32[64,64]{1,0:T(8,128)S(1)} %fusion.74), custom_call_target="Cholesky" | custom-call | tf_op jit(solution)/shard_map/jit(cholesky)/cholesky | solution.py:88
  171.4 4.9 %custom-call.10 = f32[1,64,64]{1,2,0:T(8,128)S(1)} custom-call(f32[1,64,64]{2,1,0:T(8,128)S(1)} %fusion.70), custom_call_target="InvertDiagBlocksLowerTriangular" | custom-call | tf_op jit(solution)/shard_map/triangular_solve | solution.py:54
  176.9 2.1 %fusion.15 = f32[3,64,8,128]{3,1,2,0:T(8,128)S(1)} fusion(f32[64,64,1,1]{1,0,3,2:T(8,128)S(1)} %fusion.18, f32[3,64,8,128]{1,3,2,0:T(8,128)S(1)} %get-tuple-element.8, f32[3,8,128]{2,1,0:T(8,128)S(1)} %broadcast_multiply_fusion.7), kind=kOutput, calls=%fused_computation.20 | convolution fusion | flops 151388160 | bytes 1601536 | tf_op jit(solution)/shard_map/km,fkxy->fmxy/dot_general | solution.py:93
  179.0 1.3 copy.19
  (73 shorter events, 20.3 us)
Async XLA Ops:
  1.4 8.9 %collective-permute-start.1 = (f32[2,3,128]{2,1,0:T(4,128)S(1)}, f32[2,3,128]{2,1,0:T(4,128)S(1)}, u32[]{:S(2)}, u32[]{:S(2)}) collective-permute-start(f32[2,3,128]{2,1,0:T(4,128)S(1)} %get-tuple-element.47), channel_id=1, source_target_pairs={{4,0},{8,4},{12,8},{16,12},{20,16},{24,20},{28,24},{32,28},{36,32}... | collective-permute-start | bytes 9224 | tf_op jit(solution)/shard_map/ppermute | solution.py:15
  6.5 3.8 %collective-permute-start = (f32[2,3,128]{2,1,0:T(4,128)S(1)}, f32[2,3,128]{2,1,0:T(4,128)S(1)}, u32[]{:S(2)}, u32[]{:S(2)}) collective-permute-start(f32[2,3,128]{2,1,0:T(4,128)S(1)} %get-tuple-element.46), channel_id=1, source_target_pairs={{0,4},{4,8},{8,12},{12,16},{16,20},{20,24},{24,28},{28,32},{32,36}... | collective-permute-start | bytes 9224 | tf_op jit(solution)/shard_map/ppermute | solution.py:12
  10.4 10.9 %collective-permute-start.3 = (f32[2,14,3]{2,1,0:T(8,128)S(1)}, f32[2,14,3]{2,1,0:T(8,128)S(1)}, u32[]{:S(2)}, u32[]{:S(2)}) collective-permute-start(f32[2,14,3]{2,1,0:T(8,128)S(1)} %get-tuple-element.45), channel_id=1, source_target_pairs={{1,0},{2,1},{3,2},{5,4},{6,5},{7,6},{9,8},{10,9},{11,10},{13,12},{... | collective-permute-start | bytes 1016 | tf_op jit(solution)/shard_map/ppermute | solution.py:15
  11.7 9.6 %collective-permute-start.2 = (f32[2,14,3]{2,1,0:T(8,128)S(1)}, f32[2,14,3]{2,1,0:T(8,128)S(1)}, u32[]{:S(2)}, u32[]{:S(2)}) collective-permute-start(f32[2,14,3]{2,1,0:T(8,128)S(1)} %get-tuple-element.44), channel_id=1, source_target_pairs={{0,1},{1,2},{2,3},{4,5},{5,6},{6,7},{8,9},{9,10},{10,11},{12,13},{... | collective-permute-start | bytes 1016 | tf_op jit(solution)/shard_map/ppermute | solution.py:12
  15.7 7.0 %collective-permute-start.5 = (f32[3,64,1,128]{1,3,2,0:T(8,128)S(1)}, f32[3,64,1,128]{1,3,2,0:T(8,128)S(1)}, u32[]{:S(2)}, u32[]{:S(2)}) collective-permute-start(f32[3,64,1,128]{1,3,2,0:T(8,128)S(1)} %get-tuple-element.41), channel_id=1, source_target_pairs={{4,0},{8,4},{12,8},{16,12},{20,16},{24,20},{28,24},{32,28},{36,32}... | collective-permute-start | bytes 294920 | tf_op jit(solution)/shard_map/ppermute | solution.py:15
  18.7 5.2 %collective-permute-start.4 = (f32[3,64,1,128]{1,3,2,0:T(8,128)S(1)}, f32[3,64,1,128]{1,3,2,0:T(8,128)S(1)}, u32[]{:S(2)}, u32[]{:S(2)}) collective-permute-start(f32[3,64,1,128]{1,3,2,0:T(8,128)S(1)} %get-tuple-element.40), channel_id=1, source_target_pairs={{0,4},{4,8},{8,12},{12,16},{16,20},{20,24},{24,28},{28,32},{32,36}... | collective-permute-start | bytes 294920 | tf_op jit(solution)/shard_map/ppermute | solution.py:12
  23.9 5.5 %collective-permute-start.7 = (f32[3,64,10,1]{1,3,2,0:T(1,128)S(1)}, f32[3,64,10,1]{1,3,2,0:T(1,128)S(1)}, u32[]{:S(2)}, u32[]{:S(2)}) collective-permute-start(f32[3,64,10,1]{1,3,2,0:T(1,128)S(1)} %get-tuple-element.35), channel_id=1, source_target_pairs={{1,0},{2,1},{3,2},{5,4},{6,5},{7,6},{9,8},{10,9},{11,10},{13,12},{... | collective-permute-start | bytes 23048 | tf_op jit(solution)/shard_map/ppermute | solution.py:15
  25.2 4.8 %collective-permute-start.6 = (f32[3,64,10,1]{1,3,2,0:T(1,128)S(1)}, f32[3,64,10,1]{1,3,2,0:T(1,128)S(1)}, u32[]{:S(2)}, u32[]{:S(2)}) collective-permute-start(f32[3,64,10,1]{1,3,2,0:T(1,128)S(1)} %get-tuple-element.34), channel_id=1, source_target_pairs={{0,1},{1,2},{2,3},{4,5},{5,6},{6,7},{8,9},{9,10},{10,11},{12,13},{... | collective-permute-start | bytes 23048 | tf_op jit(solution)/shard_map/ppermute | solution.py:12
  32.1 16.0 %copy-start = (s32[1,1,256]{2,1,0:T(1,128)S(1)}, s32[1,1,256]{2,1,0:T(1,128)}, u32[]{:S(2)}) copy-start(s32[1,1,256]{2,1,0:T(1,128)} %param.9) | copy-start | bytes 3076
  32.1 8.9 %collective-permute-start.9 = (f32[3,64,1,128]{1,3,2,0:T(8,128)S(1)}, f32[3,64,1,128]{1,3,2,0:T(8,128)S(1)}, u32[]{:S(2)}, u32[]{:S(2)}) collective-permute-start(f32[3,64,1,128]{1,3,2,0:T(8,128)S(1)} %get-tuple-element.39), channel_id=1, source_target_pairs={{4,0},{8,4},{12,8},{16,12},{20,16},{24,20},{28,24},{32,28},{36,32}... | collective-permute-start | bytes 294920 | tf_op jit(solution)/shard_map/ppermute | solution.py:15
  34.1 8.1 %collective-permute-start.8 = (f32[3,64,1,128]{1,3,2,0:T(8,128)S(1)}, f32[3,64,1,128]{1,3,2,0:T(8,128)S(1)}, u32[]{:S(2)}, u32[]{:S(2)}) collective-permute-start(f32[3,64,1,128]{1,3,2,0:T(8,128)S(1)} %get-tuple-element.38), channel_id=1, source_target_pairs={{0,4},{4,8},{8,12},{12,16},{16,20},{20,24},{24,28},{28,32},{32,36}... | collective-permute-start | bytes 294920 | tf_op jit(solution)/shard_map/ppermute | solution.py:12
  42.2 5.9 %collective-permute-start.11 = (f32[3,64,10,1]{1,3,2,0:T(1,128)S(1)}, f32[3,64,10,1]{1,3,2,0:T(1,128)S(1)}, u32[]{:S(2)}, u32[]{:S(2)}) collective-permute-start(f32[3,64,10,1]{1,3,2,0:T(1,128)S(1)} %get-tuple-element.33), channel_id=1, source_target_pairs={{1,0},{2,1},{3,2},{5,4},{6,5},{7,6},{9,8},{10,9},{11,10},{13,12},{... | collective-permute-start | bytes 23048 | tf_op jit(solution)/shard_map/ppermute | solution.py:15
  43.5 5.4 %collective-permute-start.10 = (f32[3,64,10,1]{1,3,2,0:T(1,128)S(1)}, f32[3,64,10,1]{1,3,2,0:T(1,128)S(1)}, u32[]{:S(2)}, u32[]{:S(2)}) collective-permute-start(f32[3,64,10,1]{1,3,2,0:T(1,128)S(1)} %get-tuple-element.32), channel_id=1, source_target_pairs={{0,1},{1,2},{2,3},{4,5},{5,6},{6,7},{8,9},{9,10},{10,11},{12,13},{... | collective-permute-start | bytes 23048 | tf_op jit(solution)/shard_map/ppermute | solution.py:12
  51.4 8.6 %collective-permute-start.13 = (f32[3,64,1,128]{1,3,2,0:T(8,128)S(1)}, f32[3,64,1,128]{1,3,2,0:T(8,128)S(1)}, u32[]{:S(2)}, u32[]{:S(2)}) collective-permute-start(f32[3,64,1,128]{1,3,2,0:T(8,128)S(1)} %get-tuple-element.37), channel_id=1, source_target_pairs={{4,0},{8,4},{12,8},{16,12},{20,16},{24,20},{28,24},{32,28},{36,32}... | collective-permute-start | bytes 294920 | tf_op jit(solution)/shard_map/ppermute | solution.py:15
  53.3 7.8 %collective-permute-start.12 = (f32[3,64,1,128]{1,3,2,0:T(8,128)S(1)}, f32[3,64,1,128]{1,3,2,0:T(8,128)S(1)}, u32[]{:S(2)}, u32[]{:S(2)}) collective-permute-start(f32[3,64,1,128]{1,3,2,0:T(8,128)S(1)} %get-tuple-element.36), channel_id=1, source_target_pairs={{0,4},{4,8},{8,12},{12,16},{16,20},{20,24},{24,28},{28,32},{32,36}... | collective-permute-start | bytes 294920 | tf_op jit(solution)/shard_map/ppermute | solution.py:12
  61.2 5.9 %collective-permute-start.15 = (f32[3,64,10,1]{1,3,2,0:T(1,128)S(1)}, f32[3,64,10,1]{1,3,2,0:T(1,128)S(1)}, u32[]{:S(2)}, u32[]{:S(2)}) collective-permute-start(f32[3,64,10,1]{1,3,2,0:T(1,128)S(1)} %get-tuple-element.31), channel_id=1, source_target_pairs={{1,0},{2,1},{3,2},{5,4},{6,5},{7,6},{9,8},{10,9},{11,10},{13,12},{... | collective-permute-start | bytes 23048 | tf_op jit(solution)/shard_map/ppermute | solution.py:15
  62.5 5.4 %collective-permute-start.14 = (f32[3,64,10,1]{1,3,2,0:T(1,128)S(1)}, f32[3,64,10,1]{1,3,2,0:T(1,128)S(1)}, u32[]{:S(2)}, u32[]{:S(2)}) collective-permute-start(f32[3,64,10,1]{1,3,2,0:T(1,128)S(1)} %get-tuple-element.30), channel_id=1, source_target_pairs={{0,1},{1,2},{2,3},{4,5},{5,6},{6,7},{8,9},{9,10},{10,11},{12,13},{... | collective-permute-start | bytes 23048 | tf_op jit(solution)/shard_map/ppermute | solution.py:12
  71.3 1.0 copy-start.1
  71.3 1.0 copy-start.2
where the time goes:
time: 181 us; the launch traced here: 180 us
  blocking collectives  91.1 us (50%)
  starting transfers between devices  49.4 us (27%)
  other arithmetic  21.6 us (12%)
  waiting for transfers between devices  9.98 us (6%)
  local copies, waits for them, and re-layouts  4.53 us (3%)
  matrix products  3.22 us (2%)
    psum x1, blocking collectives, local(): gram, projection = lax.psum((gram_part, proj_part), ('gx', 'gy'))  91.1 us
    ppermute x8, starting transfers between devices, extended(): lax.ppermute(lax.slice_in_dim(block, block.shape[dim] - width, None, axis...  32.4 us
    ppermute x8, starting transfers between devices, extended(): lax.ppermute(lax.slice_in_dim(block, 0, width, axis=dim), axis, backward)  17.1 us
    another operation x3, other arithmetic, local(): lower = jnp.linalg.cholesky(eye + gram)  6.52 us
    ppermute x8, waiting for transfers between devices, extended(): lax.ppermute(lax.slice_in_dim(block, block.shape[dim] - width, None, axis...  5.86 us
    another operation x2, other arithmetic, tri_solve(): lax.linalg.triangular_solve(lower, rhs, left_side=True, lower=True, trans...  5.55 us
    ppermute x8, waiting for transfers between devices, extended(): lax.ppermute(lax.slice_in_dim(block, 0, width, axis=dim), axis, backward)  4.11 us
  transfers between devices with their start and end apart: 16, of which 9 were waited for; matrix products, arithmetic and copies ran while one was open for 1% of the time, Pallas kernels for 0%

commit v1 on v0

--- a/solution.py
+++ b/solution.py
@@ -84,7 +84,7 @@
     gram_part = jnp.dot(scaled, scaled.T, precision=lax.Precision.HIGHEST)
     proj_part = jnp.dot(scaled, innovation, precision=lax.Precision.HIGHEST)
     eye = jnp.eye(sample_number, dtype=jnp.float32)
-    gram, projection = lax.psum((gram_part, proj_part), ("gx", "gy"))
+    gram, projection = lax.psum(lax.psum((gram_part, proj_part), "gy"), "gx")
     lower = jnp.linalg.cholesky(eye + gram)
     half = tri_solve(lower, projection[:, None], False)
     weights = tri_solve(lower, half, True)[:, 0]

time: 181 us -> 358 us (1.98)
  blocking collectives: 91.1 us -> 266 us
    psum x1 -> x2, blocking collectives: 91.1 us -> 266 us  [local(): gram, projection = lax.psum(lax.psum((gram_part, proj_part), 'gy'), 'gx')]
where the time goes in v1:
time: 358 us; the launch traced here: 355 us
  blocking collectives  266 us (74%)
  starting transfers between devices  49.4 us (14%)
  other arithmetic  21.6 us (6%)
  waiting for transfers between devices  9.98 us (3%)
  local copies, waits for them, and re-layouts  4.53 us (1%)
    psum x2, blocking collectives, local(): gram, projection = lax.psum(lax.psum((gram_part, proj_part), 'gy'), 'gx')  266 us
    ppermute x8, starting transfers between devices, extended(): lax.ppermute(lax.slice_in_dim(block, block.shape[dim] - width, None, axis...  32.4 us
    ppermute x8, starting transfers between devices, extended(): lax.ppermute(lax.slice_in_dim(block, 0, width, axis=dim), axis, backward)  17.1 us
  transfers between devices with their start and end apart: 16, of which 9 were waited for; matrix products, arithmetic and copies ran while one was open for 1% of the time, Pallas kernels for 0%

profile of v1, /device:TPU:1, one launch (start us, length us, event | category | flops | bytes accessed | tf_op | source)
XLA Modules:
  0.0 354.8 jit_solution(3783809637033234368)
XLA Ops:
  1.4 5.1 %collective-permute-start.1 = (f32[2,3,128]{2,1,0:T(4,128)S(1)}, f32[2,3,128]{2,1,0:T(4,128)S(1)}, u32[]{:S(2)}, u32[]{:S(2)}) collective-permute-start(f32[2,3,128]{2,1,0:T(4,128)S(1)} %get-tuple-element.49), channel_id=1, source_target_pairs={{4,0},{8,4},{12,8},{16,12},{20,16},{24,20},{28,24},{32,28},{36,32}... | collective-permute-start | bytes 9224 | tf_op jit(solution)/shard_map/ppermute | solution.py:15
  6.5 1.9 collective-permute-start
  8.4 1.6 copy.15
  11.7 4.0 %collective-permute-start.2 = (f32[2,14,3]{2,1,0:T(8,128)S(1)}, f32[2,14,3]{2,1,0:T(8,128)S(1)}, u32[]{:S(2)}, u32[]{:S(2)}) collective-permute-start(f32[2,14,3]{2,1,0:T(8,128)S(1)} %get-tuple-element.46), channel_id=1, source_target_pairs={{0,1},{1,2},{2,3},{4,5},{5,6},{6,7},{8,9},{9,10},{10,11},{12,13},{... | collective-permute-start | bytes 1016 | tf_op jit(solution)/shard_map/ppermute | solution.py:12
  15.7 3.0 collective-permute-start.5
  18.7 2.6 collective-permute-start.4
  21.4 1.3 collective-permute-done.5
  23.9 1.3 collective-permute-start.7
  25.2 4.0 %collective-permute-start.6 = (f32[3,64,10,1]{1,3,2,0:T(1,128)S(1)}, f32[3,64,10,1]{1,3,2,0:T(1,128)S(1)}, u32[]{:S(2)}, u32[]{:S(2)}) collective-permute-start(f32[3,64,10,1]{1,3,2,0:T(1,128)S(1)} %get-tuple-element.36), channel_id=1, source_target_pairs={{0,1},{1,2},{2,3},{4,5},{5,6},{6,7},{8,9},{9,10},{10,11},{12,13},{... | collective-permute-start | bytes 23048 | tf_op jit(solution)/shard_map/ppermute | solution.py:12
  32.1 1.9 collective-permute-start.9
  34.1 5.5 %collective-permute-start.8 = (f32[3,64,1,128]{1,3,2,0:T(8,128)S(1)}, f32[3,64,1,128]{1,3,2,0:T(8,128)S(1)}, u32[]{:S(2)}, u32[]{:S(2)}) collective-permute-start(f32[3,64,1,128]{1,3,2,0:T(8,128)S(1)} %get-tuple-element.40), channel_id=1, source_target_pairs={{0,4},{4,8},{8,12},{12,16},{16,20},{20,24},{24,28},{28,32},{32,36}... | collective-permute-start | bytes 294920 | tf_op jit(solution)/shard_map/ppermute | solution.py:12
  39.6 1.4 collective-permute-done.9
  43.5 4.5 %collective-permute-start.10 = (f32[3,64,10,1]{1,3,2,0:T(1,128)S(1)}, f32[3,64,10,1]{1,3,2,0:T(1,128)S(1)}, u32[]{:S(2)}, u32[]{:S(2)}) collective-permute-start(f32[3,64,10,1]{1,3,2,0:T(1,128)S(1)} %get-tuple-element.34), channel_id=1, source_target_pairs={{0,1},{1,2},{2,3},{4,5},{5,6},{6,7},{8,9},{9,10},{10,11},{12,13},{... | collective-permute-start | bytes 23048 | tf_op jit(solution)/shard_map/ppermute | solution.py:12
  51.4 1.9 collective-permute-start.13
  53.3 5.2 %collective-permute-start.12 = (f32[3,64,1,128]{1,3,2,0:T(8,128)S(1)}, f32[3,64,1,128]{1,3,2,0:T(8,128)S(1)}, u32[]{:S(2)}, u32[]{:S(2)}) collective-permute-start(f32[3,64,1,128]{1,3,2,0:T(8,128)S(1)} %get-tuple-element.38), channel_id=1, source_target_pairs={{0,4},{4,8},{8,12},{12,16},{16,20},{20,24},{24,28},{28,32},{32,36}... | collective-permute-start | bytes 294920 | tf_op jit(solution)/shard_map/ppermute | solution.py:12
  58.6 1.4 collective-permute-done.13
  62.5 4.5 %collective-permute-start.14 = (f32[3,64,10,1]{1,3,2,0:T(1,128)S(1)}, f32[3,64,10,1]{1,3,2,0:T(1,128)S(1)}, u32[]{:S(2)}, u32[]{:S(2)}) collective-permute-start(f32[3,64,10,1]{1,3,2,0:T(1,128)S(1)} %get-tuple-element.32), channel_id=1, source_target_pairs={{0,1},{1,2},{2,3},{4,5},{5,6},{6,7},{8,9},{9,10},{10,11},{12,13},{... | collective-permute-start | bytes 23048 | tf_op jit(solution)/shard_map/ppermute | solution.py:12
  69.5 1.7 fusion.77
  73.0 15.5 %all-reduce.1 = (f32[64,64]{1,0:T(8,128)S(1)}, f32[64]{0:T(128)S(1)}) all-reduce(f32[64,64]{1,0:T(8,128)S(1)} %fusion.83, f32[64]{0:T(128)S(1)} %convolution_bitcast_fusion.2), channel_id=1, replica_groups=mesh['gx'=64,'gy'=4] {'gy'}, use_global_device_ids=true, to_apply=%region_2.3 | all-reduce | flops 4160 | bytes 33280 | tf_op jit(solution)/shard_map/psum | solution.py:87
  88.5 250.1 %all-reduce = (f32[64,64]{1,0:T(8,128)S(1)}, f32[64]{0:T(128)S(1)}) all-reduce(f32[64,64]{1,0:T(8,128)S(1)} %get-tuple-element.7, f32[64]{0:T(128)S(1)} %get-tuple-element.8), channel_id=1, replica_groups=mesh['gx'=64,'gy'=4] {'gx'}, use_global_device_ids=true, to_apply=%region_3.4 | all-reduce | flops 4160 | bytes 33280 | tf_op jit(solution)/shard_map/psum | solution.py:87
  338.7 5.8 %cholesky.18 = f32[64,64]{1,0:T(8,128)S(1)} custom-call(f32[64,64]{1,0:T(8,128)S(1)} %fusion.74), custom_call_target="Cholesky" | custom-call | tf_op jit(solution)/shard_map/jit(cholesky)/cholesky | solution.py:88
  345.9 4.9 %custom-call.10 = f32[1,64,64]{1,2,0:T(8,128)S(1)} custom-call(f32[1,64,64]{2,1,0:T(8,128)S(1)} %fusion.70), custom_call_target="InvertDiagBlocksLowerTriangular" | custom-call | tf_op jit(solution)/shard_map/triangular_solve | solution.py:54
  351.3 2.1 fusion.15
  353.5 1.3 copy.19
  (74 shorter events, 21.6 us)
Async XLA Ops:
  1.4 8.9 %collective-permute-start.1 = (f32[2,3,128]{2,1,0:T(4,128)S(1)}, f32[2,3,128]{2,1,0:T(4,128)S(1)}, u32[]{:S(2)}, u32[]{:S(2)}) collective-permute-start(f32[2,3,128]{2,1,0:T(4,128)S(1)} %get-tuple-element.49), channel_id=1, source_target_pairs={{4,0},{8,4},{12,8},{16,12},{20,16},{24,20},{28,24},{32,28},{36,32}... | collective-permute-start | bytes 9224 | tf_op jit(solution)/shard_map/ppermute | solution.py:15
  6.5 3.8 %collective-permute-start = (f32[2,3,128]{2,1,0:T(4,128)S(1)}, f32[2,3,128]{2,1,0:T(4,128)S(1)}, u32[]{:S(2)}, u32[]{:S(2)}) collective-permute-start(f32[2,3,128]{2,1,0:T(4,128)S(1)} %get-tuple-element.48), channel_id=1, source_target_pairs={{0,4},{4,8},{8,12},{12,16},{16,20},{20,24},{24,28},{28,32},{32,36}... | collective-permute-start | bytes 9224 | tf_op jit(solution)/shard_map/ppermute | solution.py:12
  10.4 10.9 %collective-permute-start.3 = (f32[2,14,3]{2,1,0:T(8,128)S(1)}, f32[2,14,3]{2,1,0:T(8,128)S(1)}, u32[]{:S(2)}, u32[]{:S(2)}) collective-permute-start(f32[2,14,3]{2,1,0:T(8,128)S(1)} %get-tuple-element.47), channel_id=1, source_target_pairs={{1,0},{2,1},{3,2},{5,4},{6,5},{7,6},{9,8},{10,9},{11,10},{13,12},{... | collective-permute-start | bytes 1016 | tf_op jit(solution)/shard_map/ppermute | solution.py:15
  11.7 9.6 %collective-permute-start.2 = (f32[2,14,3]{2,1,0:T(8,128)S(1)}, f32[2,14,3]{2,1,0:T(8,128)S(1)}, u32[]{:S(2)}, u32[]{:S(2)}) collective-permute-start(f32[2,14,3]{2,1,0:T(8,128)S(1)} %get-tuple-element.46), channel_id=1, source_target_pairs={{0,1},{1,2},{2,3},{4,5},{5,6},{6,7},{8,9},{9,10},{10,11},{12,13},{... | collective-permute-start | bytes 1016 | tf_op jit(solution)/shard_map/ppermute | solution.py:12
  15.7 7.0 %collective-permute-start.5 = (f32[3,64,1,128]{1,3,2,0:T(8,128)S(1)}, f32[3,64,1,128]{1,3,2,0:T(8,128)S(1)}, u32[]{:S(2)}, u32[]{:S(2)}) collective-permute-start(f32[3,64,1,128]{1,3,2,0:T(8,128)S(1)} %get-tuple-element.43), channel_id=1, source_target_pairs={{4,0},{8,4},{12,8},{16,12},{20,16},{24,20},{28,24},{32,28},{36,32}... | collective-permute-start | bytes 294920 | tf_op jit(solution)/shard_map/ppermute | solution.py:15
  18.7 5.2 %collective-permute-start.4 = (f32[3,64,1,128]{1,3,2,0:T(8,128)S(1)}, f32[3,64,1,128]{1,3,2,0:T(8,128)S(1)}, u32[]{:S(2)}, u32[]{:S(2)}) collective-permute-start(f32[3,64,1,128]{1,3,2,0:T(8,128)S(1)} %get-tuple-element.42), channel_id=1, source_target_pairs={{0,4},{4,8},{8,12},{12,16},{16,20},{20,24},{24,28},{28,32},{32,36}... | collective-permute-start | bytes 294920 | tf_op jit(solution)/shard_map/ppermute | solution.py:12
  23.9 5.5 %collective-permute-start.7 = (f32[3,64,10,1]{1,3,2,0:T(1,128)S(1)}, f32[3,64,10,1]{1,3,2,0:T(1,128)S(1)}, u32[]{:S(2)}, u32[]{:S(2)}) collective-permute-start(f32[3,64,10,1]{1,3,2,0:T(1,128)S(1)} %get-tuple-element.37), channel_id=1, source_target_pairs={{1,0},{2,1},{3,2},{5,4},{6,5},{7,6},{9,8},{10,9},{11,10},{13,12},{... | collective-permute-start | bytes 23048 | tf_op jit(solution)/shard_map/ppermute | solution.py:15
  25.2 4.8 %collective-permute-start.6 = (f32[3,64,10,1]{1,3,2,0:T(1,128)S(1)}, f32[3,64,10,1]{1,3,2,0:T(1,128)S(1)}, u32[]{:S(2)}, u32[]{:S(2)}) collective-permute-start(f32[3,64,10,1]{1,3,2,0:T(1,128)S(1)} %get-tuple-element.36), channel_id=1, source_target_pairs={{0,1},{1,2},{2,3},{4,5},{5,6},{6,7},{8,9},{9,10},{10,11},{12,13},{... | collective-permute-start | bytes 23048 | tf_op jit(solution)/shard_map/ppermute | solution.py:12
  32.1 16.0 %copy-start = (s32[1,1,256]{2,1,0:T(1,128)S(1)}, s32[1,1,256]{2,1,0:T(1,128)}, u32[]{:S(2)}) copy-start(s32[1,1,256]{2,1,0:T(1,128)} %param.9) | copy-start | bytes 3076
  32.1 8.9 %collective-permute-start.9 = (f32[3,64,1,128]{1,3,2,0:T(8,128)S(1)}, f32[3,64,1,128]{1,3,2,0:T(8,128)S(1)}, u32[]{:S(2)}, u32[]{:S(2)}) collective-permute-start(f32[3,64,1,128]{1,3,2,0:T(8,128)S(1)} %get-tuple-element.41), channel_id=1, source_target_pairs={{4,0},{8,4},{12,8},{16,12},{20,16},{24,20},{28,24},{32,28},{36,32}... | collective-permute-start | bytes 294920 | tf_op jit(solution)/shard_map/ppermute | solution.py:15
  34.1 8.1 %collective-permute-start.8 = (f32[3,64,1,128]{1,3,2,0:T(8,128)S(1)}, f32[3,64,1,128]{1,3,2,0:T(8,128)S(1)}, u32[]{:S(2)}, u32[]{:S(2)}) collective-permute-start(f32[3,64,1,128]{1,3,2,0:T(8,128)S(1)} %get-tuple-element.40), channel_id=1, source_target_pairs={{0,4},{4,8},{8,12},{12,16},{16,20},{20,24},{24,28},{28,32},{32,36}... | collective-permute-start | bytes 294920 | tf_op jit(solution)/shard_map/ppermute | solution.py:12
  42.2 5.9 %collective-permute-start.11 = (f32[3,64,10,1]{1,3,2,0:T(1,128)S(1)}, f32[3,64,10,1]{1,3,2,0:T(1,128)S(1)}, u32[]{:S(2)}, u32[]{:S(2)}) collective-permute-start(f32[3,64,10,1]{1,3,2,0:T(1,128)S(1)} %get-tuple-element.35), channel_id=1, source_target_pairs={{1,0},{2,1},{3,2},{5,4},{6,5},{7,6},{9,8},{10,9},{11,10},{13,12},{... | collective-permute-start | bytes 23048 | tf_op jit(solution)/shard_map/ppermute | solution.py:15
  43.5 5.4 %collective-permute-start.10 = (f32[3,64,10,1]{1,3,2,0:T(1,128)S(1)}, f32[3,64,10,1]{1,3,2,0:T(1,128)S(1)}, u32[]{:S(2)}, u32[]{:S(2)}) collective-permute-start(f32[3,64,10,1]{1,3,2,0:T(1,128)S(1)} %get-tuple-element.34), channel_id=1, source_target_pairs={{0,1},{1,2},{2,3},{4,5},{5,6},{6,7},{8,9},{9,10},{10,11},{12,13},{... | collective-permute-start | bytes 23048 | tf_op jit(solution)/shard_map/ppermute | solution.py:12
  51.4 8.6 %collective-permute-start.13 = (f32[3,64,1,128]{1,3,2,0:T(8,128)S(1)}, f32[3,64,1,128]{1,3,2,0:T(8,128)S(1)}, u32[]{:S(2)}, u32[]{:S(2)}) collective-permute-start(f32[3,64,1,128]{1,3,2,0:T(8,128)S(1)} %get-tuple-element.39), channel_id=1, source_target_pairs={{4,0},{8,4},{12,8},{16,12},{20,16},{24,20},{28,24},{32,28},{36,32}... | collective-permute-start | bytes 294920 | tf_op jit(solution)/shard_map/ppermute | solution.py:15
  53.3 7.8 %collective-permute-start.12 = (f32[3,64,1,128]{1,3,2,0:T(8,128)S(1)}, f32[3,64,1,128]{1,3,2,0:T(8,128)S(1)}, u32[]{:S(2)}, u32[]{:S(2)}) collective-permute-start(f32[3,64,1,128]{1,3,2,0:T(8,128)S(1)} %get-tuple-element.38), channel_id=1, source_target_pairs={{0,4},{4,8},{8,12},{12,16},{16,20},{20,24},{24,28},{28,32},{32,36}... | collective-permute-start | bytes 294920 | tf_op jit(solution)/shard_map/ppermute | solution.py:12
  61.2 5.9 %collective-permute-start.15 = (f32[3,64,10,1]{1,3,2,0:T(1,128)S(1)}, f32[3,64,10,1]{1,3,2,0:T(1,128)S(1)}, u32[]{:S(2)}, u32[]{:S(2)}) collective-permute-start(f32[3,64,10,1]{1,3,2,0:T(1,128)S(1)} %get-tuple-element.33), channel_id=1, source_target_pairs={{1,0},{2,1},{3,2},{5,4},{6,5},{7,6},{9,8},{10,9},{11,10},{13,12},{... | collective-permute-start | bytes 23048 | tf_op jit(solution)/shard_map/ppermute | solution.py:15
  62.5 5.4 %collective-permute-start.14 = (f32[3,64,10,1]{1,3,2,0:T(1,128)S(1)}, f32[3,64,10,1]{1,3,2,0:T(1,128)S(1)}, u32[]{:S(2)}, u32[]{:S(2)}) collective-permute-start(f32[3,64,10,1]{1,3,2,0:T(1,128)S(1)} %get-tuple-element.32), channel_id=1, source_target_pairs={{0,1},{1,2},{2,3},{4,5},{5,6},{6,7},{8,9},{9,10},{10,11},{12,13},{... | collective-permute-start | bytes 23048 | tf_op jit(solution)/shard_map/ppermute | solution.py:12
  71.3 1.0 copy-start.1
  71.3 1.0 copy-start.2
